TPU v7x, 256 devices: a whole 4x4x8 slice. The times are simulated.
256 devices in a mesh: track: 16 (over z, x_lo), tm: 16 (over x_hi, y, core).
Axes of the slice: x: 4 (x_hi: 2, x_lo: 2; x = x_hi * 2 + x_lo), y: 4, z: 8, core: 2. Of those that a mesh axis runs over, the one named last changes fastest.
Arguments:
- positions: float32 [3, 32, 6144], P(None, 'tm', 'track'), may hold values from -6 to 6
- embeddings: float32 [32, 128, 6144], P('tm', None, 'track'), may hold values from -6 to 6
- visible: int32 [32, 6144], P('tm', 'track'), may hold values 0 or 1
Outputs:
- grad_positions: float32 [3, 32, 6144], P(None, 'tm', 'track')
- grad_embeddings: float32 [32, 128, 6144], P('tm', None, 'track')
- mean_loss: float32 [], replicated
All inputs are finite; a program needn't handle non-finite values. No bound on the sum of `visible` on one device may be relied on, other than what follows from the above.
Results may differ from a plain program's by a relative error of at most 0.00014.
Values sent between devices are 32-bit elements; how exact they have to be, the bound alone decides.
A program may use at most 128 MiB of HBM per device.

v0:
```python
import math
import jax
import jax.numpy as jnp
from jax import lax
from jax.sharding import PartitionSpec as P

rigidity = 4.0
highest = lax.Precision.HIGHEST


def shifted(array, axis, by):
    size = lax.axis_size(axis)
    pairs = [(i, i + by) for i in range(size) if 0 <= i + by < size]
    return lax.ppermute(array, axis, pairs)


def tile_terms(pos_a, mask_a, emb_a, pos_b, mask_b, emb_b, weight_scale):
    inv_root = 1.0 / math.sqrt(emb_a.shape[1])
    offset = pos_a[:, :, :, None] - pos_b[:, :, None, :]
    distance = jnp.sqrt(jnp.sum(offset * offset, axis=0) + 1.0)
    change = distance[1:] - distance[:-1]
    both_seen = mask_a[:, :, None] * mask_b[:, None, :]
    seen_pair = both_seen[1:] * both_seen[:-1]
    logits = jnp.einsum("fei,fej->fij", emb_a, emb_b, precision=highest) * inv_root
    affinity = jax.nn.sigmoid(logits)
    squared = seen_pair * change * change
    energy = jnp.sum(affinity * squared)
    grad_change = 2.0 * weight_scale * affinity * seen_pair * change
    padding = jnp.zeros_like(grad_change[:1])
    grad_dist = jnp.concatenate([padding, grad_change], 0) - jnp.concatenate(
        [grad_change, padding], 0
    )
    scaled = (grad_dist / distance)[None] * offset
    grad_pos_a = jnp.sum(scaled, axis=3)
    grad_pos_b = -jnp.sum(scaled, axis=2)
    grad_logit = weight_scale * squared * affinity * (1.0 - affinity) * inv_root
    grad_emb_a = jnp.einsum("fij,fej->fei", grad_logit, emb_b, precision=highest)
    grad_emb_b = jnp.einsum("fij,fei->fej", grad_logit, emb_a, precision=highest)
    return (energy, grad_pos_a, grad_emb_a, grad_pos_b, grad_emb_b)


def on_device(positions, embeddings, visible):
    frames_local = embeddings.shape[0]
    block_width = embeddings.shape[2]
    tracks = block_width * lax.axis_size("track")
    frames = frames_local * lax.axis_size("tm")
    weight_scale = rigidity / math.sqrt(tracks)
    seen_mask = visible.astype(jnp.float32)
    next_pos, next_mask = shifted((positions[:, :1], seen_mask[:1]), "tm", -1)
    pos_ext = jnp.concatenate([positions, next_pos], 1)
    mask_ext = jnp.concatenate([seen_mask, next_mask], 0)
    packed = jnp.concatenate([pos_ext, mask_ext[None]], 0)

    def own_tile(others_packed, others_emb):
        return tile_terms(
            pos_ext,
            mask_ext,
            embeddings,
            others_packed[:3],
            others_packed[3],
            others_emb,
            weight_scale,
        )

    initial = (jnp.zeros_like(pos_ext), jnp.zeros_like(embeddings), jnp.zeros((), jnp.float32))
    piece_packed = lax.all_gather(packed, "track", axis=2, tiled=True)
    piece_emb = lax.all_gather(embeddings, "track", axis=2, tiled=True)
    columns = piece_emb.shape[2]
    blocks = columns // block_width
    split_packed = jnp.moveaxis(
        piece_packed.reshape(4, frames_local + 1, blocks, block_width), 2, 0
    )
    split_emb = jnp.moveaxis(
        piece_emb.reshape(frames_local, piece_emb.shape[1], blocks, block_width), 2, 0
    )

    def advance(inner, others):
        energy, grad_pos_a, grad_emb_a, unused_pos, unused_emb = own_tile(others[0], others[1])
        return ((inner[0] + grad_pos_a, inner[1] + grad_emb_a, inner[2] + energy), None)

    result, unused = lax.scan(advance, initial, (split_packed, split_emb))
    grad_pos, grad_emb, energy_sum = result
    energy_sum = 0.5 * energy_sum
    incoming = shifted(grad_pos[:, -1:], "tm", 1)
    grad_positions = grad_pos[:, :-1]
    grad_positions = jnp.concatenate([grad_positions[:, :1] + incoming, grad_positions[:, 1:]], 1)
    total = lax.psum(energy_sum, ("track", "tm"))
    mean_loss = total / (tracks * (tracks - 1) / 2.0 * (frames - 1))
    return (grad_positions, grad_emb, mean_loss)


def solution(mesh):
    in_specs = (P(None, "tm", "track"), P("tm", None, "track"), P("tm", "track"))
    out_specs = (P(None, "tm", "track"), P("tm", None, "track"), P())
    return jax.shard_map(
        on_device, mesh=mesh, in_specs=in_specs, out_specs=out_specs, check_vma=False
    )
```

profile of v0, /device:TPU:1, one launch (start us, length us, event | category | flops | bytes accessed | tf_op | source)
XLA Modules:
  0.0 581.3 jit_solution(791380038999158030)
XLA Ops:
  7.2 1.9 copy.30
  9.9 5.1 collective-permute-start
  15.7 1.9 collective-permute-start.1
  17.6 3.0 collective-permute-done.1
  21.3 41.1 %all_gather.7 = f32[4,3,6144]{2,1,0:T(4,128)S(1)} all-gather(f32[4,3,384]{2,1,0:T(4,128)S(1)} %pad_maximum_fusion), channel_id=1, replica_groups=mesh['track'=16,'tm'=16] {'track'}, dimensions={2}, use_global_device_ids=true | all-gather | bytes 313344 | tf_op jit(solution)/shard_map/all_gather | solution.py:66
  63.9 97.0 %all-gather.2.cloned.1.call-done = f32[2,128,6144]{1,2,0:T(8,128)} async-done(((f32[2,128,384]{1,2,0:T(8,128)}), f32[2,128,6144]{1,2,0:T(8,128)}) %all-gather.2.cloned.1.call-update) | async-done | bytes 6291472 | tf_op jit(solution)/shard_map/all_gather | solution.py:67
  160.9 327.7 %while.15 = (s32[]{:T(128)}, f32[3,3,384]{2,1,0:T(4,128)}, f32[2,128,384]{2,1,0:T(8,128)}, f32[]{:T(128)}, f32[16,2,128,384]{2,3,0,1:T(8,128)}, /*index=5*/f32[2...) while((s32[]{:T(128)}, f32[3,3,384]{2,1,0:T(4,128)}, ...), condition=%wide.region_4.5_spmd.clone, body=%wide.region_0.4_spmd.clone.sunk | while | flops 922389888 | bytes 49315164 | solution.py:81
  167.0 5.0 multiply_reduce_fusion.2
  172.7 4.3 convolution_add_fusion.2
  187.4 5.0 multiply_reduce_fusion.2
  193.2 4.4 convolution_add_fusion.2
  207.9 5.0 multiply_reduce_fusion.2
  213.6 4.4 convolution_add_fusion.2
  219.9 1.8 fusion.35
  228.4 5.0 multiply_reduce_fusion.2
  234.1 4.4 convolution_add_fusion.2
  248.9 5.0 multiply_reduce_fusion.2
  254.6 4.4 convolution_add_fusion.2
  260.9 1.8 fusion.35
  269.4 5.0 multiply_reduce_fusion.2
  275.1 4.4 convolution_add_fusion.2
  281.3 1.8 fusion.35
  289.9 5.0 multiply_reduce_fusion.2
  295.6 4.4 convolution_add_fusion.2
  310.3 5.0 multiply_reduce_fusion.2
  316.1 4.4 convolution_add_fusion.2
  322.3 1.8 fusion.35
  330.8 5.0 multiply_reduce_fusion.2
  336.6 4.4 convolution_add_fusion.2
  351.3 5.0 multiply_reduce_fusion.2
  357.1 4.4 convolution_add_fusion.2
  363.3 1.8 fusion.35
  371.8 5.0 multiply_reduce_fusion.2
  377.5 4.4 convolution_add_fusion.2
  383.8 1.8 fusion.35
  392.3 5.0 multiply_reduce_fusion.2
  398.0 4.4 convolution_add_fusion.2
  404.3 1.8 fusion.35
  412.8 5.0 multiply_reduce_fusion.2
  418.5 4.4 convolution_add_fusion.2
  433.3 5.0 multiply_reduce_fusion.2
  439.0 4.4 convolution_add_fusion.2
  453.7 5.0 multiply_reduce_fusion.2
  459.5 4.4 convolution_add_fusion.2
  474.2 5.0 multiply_reduce_fusion.2
  480.0 4.4 convolution_add_fusion.2
  489.4 4.8 collective-permute-start.2
  494.2 77.0 %psum.7 = f32[]{:T(128)} all-reduce(f32[]{:T(128)S(6)} %mul_shard_map.3), channel_id=1, replica_groups=mesh['track'=16,'tm'=16] {'track','tm'}, use_global_device_ids=true, to_apply=%region_5.6 | all-reduce | flops 1 | bytes 8 | tf_op jit(solution)/shard_map/psum | solution.py:87
  (379 shorter events, 157.2 us)
Async XLA Ops:
  7.2 56.1 %copy-start.6 = (f32[3,2,384]{2,1,0:T(2,128)S(1)}, f32[3,2,384]{2,1,0:T(2,128)}, u32[]{:S(2)}) copy-start(f32[3,2,384]{2,1,0:T(2,128)} %param.5) | copy-start | bytes 27652
  7.2 153.8 %all-gather.2.cloned.1.call-start = ((), (), s32[]{:S(2)}) async-start(), calls=%async_computation | async-start | bytes 6684672 | tf_op jit(solution)/shard_map/all_gather | solution.py:67
  9.9 7.7 %collective-permute-start = (f32[1,384]{1,0:T(1,128)S(1)}, f32[1,384]{1,0:T(1,128)S(1)}, u32[]{:S(2)}, u32[]{:S(2)}) collective-permute-start(f32[1,384]{1,0:T(1,128)S(1)} %slice.53), channel_id=1, source_target_pairs={{1,0},{2,1},{3,2},{4,3},{5,4},{6,5},{7,6},{8,7},{9,8},{10,9},{11,1... | collective-permute-start | bytes 4616 | tf_op jit(solution)/shard_map/ppermute | solution.py:14
  15.7 4.9 collective-permute-start.1
  166.7 5.4 copy-start
  172.7 4.3 copy-start.1
  178.9 1.8 copy-start.3
  187.1 5.4 copy-start
  193.1 4.4 copy-start.1
  207.6 5.4 copy-start
  213.6 4.4 copy-start.1
  219.9 1.8 copy-start.3
  228.0 5.4 copy-start
  234.1 4.4 copy-start.1
  248.5 5.4 copy-start
  254.6 4.4 copy-start.1
  260.8 1.8 copy-start.3
  269.0 5.4 copy-start
  275.1 4.4 copy-start.1
  281.3 1.8 copy-start.3
  289.5 5.4 copy-start
  295.6 4.4 copy-start.1
  301.8 1.8 copy-start.3
  310.0 5.4 copy-start
  316.1 4.4 copy-start.1
  322.3 1.8 copy-start.3
  330.5 5.4 copy-start
  336.6 4.4 copy-start.1
  342.8 1.8 copy-start.3
  351.0 5.4 copy-start
  357.0 4.4 copy-start.1
  363.3 1.8 copy-start.3
  371.4 5.4 copy-start
  377.5 4.4 copy-start.1
  383.8 1.8 copy-start.3
  391.9 5.4 copy-start
  398.0 4.4 copy-start.1
  404.3 1.8 copy-start.3
  412.4 5.4 copy-start
  418.5 4.4 copy-start.1
  432.9 5.4 copy-start
  439.0 4.4 copy-start.1
  445.2 1.8 copy-start.3
  453.4 5.4 copy-start
  459.5 4.4 copy-start.1
  473.9 5.4 copy-start
  480.0 4.4 copy-start.1
  489.4 82.5 %collective-permute-start.2 = (f32[3,1,384]{2,1,0:T(1,128)S(1)}, f32[3,1,384]{2,1,0:T(1,128)S(1)}, u32[]{:S(2)}, u32[]{:S(2)}) collective-permute-start(f32[3,1,384]{2,1,0:T(1,128)S(1)} %slice.41), channel_id=1, source_target_pairs={{0,1},{1,2},{2,3},{3,4},{4,5},{5,6},{6,7},{7,8},{8,9},{9,10},{10,1... | collective-permute-start | bytes 13832 | tf_op jit(solution)/shard_map/ppermute | solution.py:14
  (53 other events, 44.3 us)
Sparse Core Ops, SparseCore 0:
  9.8 151.1 all-gather.1
where the time goes:
time: 586 us; the launch traced here: 581 us
  matrix products  151 us (26%)
  blocking collectives  118 us (20%)
  waiting for transfers between devices  100 us (17%)
  local copies, waits for them, and re-layouts  94.3 us (16%)
  other arithmetic  77.4 us (13%)
  between operations  15.9 us (3%)
  loops' own time  12.7 us (2%)
  starting transfers between devices  11.9 us (2%)
    all_gather x1, waiting for transfers between devices, on_device(): piece_emb = lax.all_gather(embeddings, 'track', axis=2, tiled=True)  97 us
    dot_general x16, matrix products, tile_terms(): jnp.einsum('fei,fej->fij', emb_a, emb_b, precision=highest) * inv_root  80.6 us
    psum x1, blocking collectives, on_device(): total = lax.psum(energy_sum, ('track', 'tm'))  77 us
    dot_general x16, matrix products, tile_terms(): jnp.einsum('fij,fej->fei', grad_logit, emb_b, precision=highest)  70.5 us
    all_gather x1, blocking collectives, on_device(): piece_packed = lax.all_gather(packed, 'track', axis=2, tiled=True)  41.1 us
    reduce_sum x16, other arithmetic, tile_terms(): grad_pos_a = jnp.sum(scaled, axis=3)  28.8 us
    while x224, local copies, waits for them, and re-layouts  24.9 us
    reduce_sum x16, other arithmetic, tile_terms(): distance = jnp.sqrt(jnp.sum(offset * offset, axis=0) + 1.0)  24.9 us
  transfers between devices with their start and end apart: 4, of which 2 were waited for; matrix products, arithmetic and copies ran while one was open for 1% of the time, Pallas kernels for 0%

commit v1 on v0

--- a/solution.py
+++ b/solution.py
@@ -6,6 +6,11 @@
 
 rigidity = 4.0
 highest = lax.Precision.HIGHEST
+
+
+def by_each_axis(value, one, other):
+    half = lax.psum(value, one)
+    return lax.psum(half, other)
 
 
 def shifted(array, axis, by):
@@ -84,7 +89,7 @@
     incoming = shifted(grad_pos[:, -1:], "tm", 1)
     grad_positions = grad_pos[:, :-1]
     grad_positions = jnp.concatenate([grad_positions[:, :1] + incoming, grad_positions[:, 1:]], 1)
-    total = lax.psum(energy_sum, ("track", "tm"))
+    total = by_each_axis(energy_sum, "tm", "track")
     mean_loss = total / (tracks * (tracks - 1) / 2.0 * (frames - 1))
     return (grad_positions, grad_emb, mean_loss)
 

time: 586 us -> 576 us (0.983)
  the two profiles are of different devices: /device:TPU:1 before, /device:TPU:4 now
where the time goes in v1:
time: 576 us; the launch traced here: 571 us
  matrix products  150 us (26%)
  blocking collectives  121 us (21%)
  local copies, waits for them, and re-layouts  94.2 us (16%)
  waiting for transfers between devices  93.5 us (16%)
  other arithmetic  77.4 us (13%)
  between operations  15.9 us (3%)
  loops' own time  10.9 us (2%)
  starting transfers between devices  8.81 us (2%)
    all_gather x1, waiting for transfers between devices, on_device(): piece_emb = lax.all_gather(embeddings, 'track', axis=2, tiled=True)  92.2 us
    dot_general x16, matrix products, tile_terms(): jnp.einsum('fei,fej->fij', emb_a, emb_b, precision=highest) * inv_root  79.7 us
    dot_general x16, matrix products, tile_terms(): jnp.einsum('fij,fej->fei', grad_logit, emb_b, precision=highest)  70.5 us
    all_gather x1, blocking collectives, on_device(): piece_packed = lax.all_gather(packed, 'track', axis=2, tiled=True)  48.1 us
    psum x1, blocking collectives, by_each_axis(): half = lax.psum(value, one)  39 us
    psum x1, blocking collectives, by_each_axis(): return lax.psum(half, other)  33.6 us
    reduce_sum x16, other arithmetic, tile_terms(): grad_pos_a = jnp.sum(scaled, axis=3)  28.8 us
    reduce_sum x16, other arithmetic, tile_terms(): distance = jnp.sqrt(jnp.sum(offset * offset, axis=0) + 1.0)  24.9 us
  transfers between devices with their start and end apart: 4, of which 2 were waited for; matrix products, arithmetic and copies ran while one was open for 1% of the time, Pallas kernels for 0%

profile of v1, /device:TPU:4, one launch (start us, length us, event | category | flops | bytes accessed | tf_op | source)
XLA Modules:
  0.0 571.5 jit_solution(14296015788549141379)
XLA Ops:
  7.2 1.9 copy.30
  9.8 4.3 collective-permute-start
  14.9 2.6 collective-permute-start.1
  19.5 48.1 %all_gather.7 = f32[4,3,6144]{2,1,0:T(4,128)S(1)} all-gather(f32[4,3,384]{2,1,0:T(4,128)S(1)} %pad_maximum_fusion), channel_id=1, replica_groups=mesh['track'=16,'tm'=16] {'track'}, dimensions={2}, use_global_device_ids=true | all-gather | bytes 313344 | tf_op jit(solution)/shard_map/all_gather | solution.py:71
  69.1 92.2 %all-gather.2.cloned.1.call-done = f32[2,128,6144]{1,2,0:T(8,128)} async-done(((f32[2,128,384]{1,2,0:T(8,128)}), f32[2,128,6144]{1,2,0:T(8,128)}) %all-gather.2.cloned.1.call-update) | async-done | bytes 6291472 | tf_op jit(solution)/shard_map/all_gather | solution.py:72
  161.3 324.9 %while.15 = (s32[]{:T(128)}, f32[3,3,384]{2,1,0:T(4,128)}, f32[2,128,384]{2,1,0:T(8,128)}, f32[]{:T(128)}, f32[16,2,128,384]{2,3,0,1:T(8,128)}, /*index=5*/f32[2...) while((s32[]{:T(128)}, f32[3,3,384]{2,1,0:T(4,128)}, ...), condition=%wide.region_4.5_spmd.clone, body=%wide.region_0.4_spmd.clone.sunk | while | flops 922389888 | bytes 49315164 | solution.py:86
  167.3 5.0 multiply_reduce_fusion.2
  172.9 4.3 convolution_add_fusion.2
  187.6 5.0 multiply_reduce_fusion.2
  193.1 4.4 convolution_add_fusion.2
  207.9 5.0 multiply_reduce_fusion.2
  213.4 4.4 convolution_add_fusion.2
  228.2 5.0 multiply_reduce_fusion.2
  233.7 4.4 convolution_add_fusion.2
  240.0 1.8 fusion.35
  248.5 5.0 multiply_reduce_fusion.2
  254.1 4.4 convolution_add_fusion.2
  260.3 1.8 fusion.35
  268.8 5.0 multiply_reduce_fusion.2
  274.4 4.4 convolution_add_fusion.2
  280.6 1.8 fusion.35
  289.1 5.0 multiply_reduce_fusion.2
  294.7 4.4 convolution_add_fusion.2
  300.9 1.8 fusion.35
  309.4 5.0 multiply_reduce_fusion.2
  315.0 4.4 convolution_add_fusion.2
  321.2 1.8 fusion.35
  329.7 5.0 multiply_reduce_fusion.2
  335.3 4.4 convolution_add_fusion.2
  341.5 1.8 fusion.35
  350.0 5.0 multiply_reduce_fusion.2
  355.6 4.4 convolution_add_fusion.2
  361.9 1.8 fusion.35
  370.4 5.0 multiply_reduce_fusion.2
  375.9 4.4 convolution_add_fusion.2
  390.7 5.0 multiply_reduce_fusion.2
  396.2 4.4 convolution_add_fusion.2
  411.0 5.0 multiply_reduce_fusion.2
  416.5 4.4 convolution_add_fusion.2
  431.3 5.0 multiply_reduce_fusion.2
  436.9 4.4 convolution_add_fusion.2
  451.6 5.0 multiply_reduce_fusion.2
  457.2 4.4 convolution_add_fusion.2
  471.9 5.0 multiply_reduce_fusion.2
  477.5 4.4 convolution_add_fusion.2
  486.9 1.9 collective-permute-start.2
  488.8 39.0 %psum.14 = f32[]{:T(128)} all-reduce(f32[]{:T(128)S(6)} %mul_shard_map.3), channel_id=1, replica_groups=mesh['track'=16,'tm'=16] {'tm'}, use_global_device_ids=true, to_apply=%region_5.6 | all-reduce | flops 1 | bytes 8 | tf_op jit(solution)/shard_map/psum | solution.py:12
  527.8 33.6 %psum.15 = f32[]{:T(128)} all-reduce(f32[]{:T(128)} %psum.14), channel_id=1, replica_groups=mesh['track'=16,'tm'=16] {'track'}, use_global_device_ids=true, to_apply=%region_6.7 | all-reduce | flops 1 | bytes 8 | tf_op jit(solution)/shard_map/psum | solution.py:13
  (380 shorter events, 158.4 us)
Async XLA Ops:
  7.2 61.3 %copy-start.6 = (f32[3,2,384]{2,1,0:T(2,128)S(1)}, f32[3,2,384]{2,1,0:T(2,128)}, u32[]{:S(2)}) copy-start(f32[3,2,384]{2,1,0:T(2,128)} %param.5) | copy-start | bytes 27652
  7.2 154.1 %all-gather.2.cloned.1.call-start = ((), (), s32[]{:S(2)}) async-start(), calls=%async_computation | async-start | bytes 6684672 | tf_op jit(solution)/shard_map/all_gather | solution.py:72
  9.8 7.6 %collective-permute-start = (f32[1,384]{1,0:T(1,128)S(1)}, f32[1,384]{1,0:T(1,128)S(1)}, u32[]{:S(2)}, u32[]{:S(2)}) collective-permute-start(f32[1,384]{1,0:T(1,128)S(1)} %slice.53), channel_id=1, source_target_pairs={{1,0},{2,1},{3,2},{4,3},{5,4},{6,5},{7,6},{8,7},{9,8},{10,9},{11,1... | collective-permute-start | bytes 4616 | tf_op jit(solution)/shard_map/ppermute | solution.py:19
  14.9 3.9 collective-permute-start.1
  167.0 5.3 copy-start
  172.9 4.3 copy-start.1
  187.2 5.3 copy-start
  193.1 4.4 copy-start.1
  207.5 5.3 copy-start
  213.4 4.4 copy-start.1
  227.8 5.3 copy-start
  233.7 4.4 copy-start.1
  240.0 1.8 copy-start.3
  248.1 5.3 copy-start
  254.0 4.4 copy-start.1
  260.3 1.8 copy-start.3
  268.4 5.3 copy-start
  274.4 4.4 copy-start.1
  280.6 1.8 copy-start.3
  288.8 5.3 copy-start
  294.7 4.4 copy-start.1
  300.9 1.8 copy-start.3
  309.1 5.3 copy-start
  315.0 4.4 copy-start.1
  321.2 1.8 copy-start.3
  329.4 5.3 copy-start
  335.3 4.4 copy-start.1
  341.5 1.8 copy-start.3
  349.7 5.3 copy-start
  355.6 4.4 copy-start.1
  361.8 1.8 copy-start.3
  370.0 5.3 copy-start
  375.9 4.4 copy-start.1
  382.2 1.8 copy-start.3
  390.3 5.3 copy-start
  396.2 4.4 copy-start.1
  402.5 1.8 copy-start.3
  410.6 5.3 copy-start
  416.5 4.4 copy-start.1
  422.8 1.8 copy-start.3
  430.9 5.3 copy-start
  436.8 4.4 copy-start.1
  443.1 1.8 copy-start.3
  451.3 5.3 copy-start
  457.2 4.4 copy-start.1
  471.6 5.3 copy-start
  477.5 4.4 copy-start.1
  486.9 75.2 %collective-permute-start.2 = (f32[3,1,384]{2,1,0:T(1,128)S(1)}, f32[3,1,384]{2,1,0:T(1,128)S(1)}, u32[]{:S(2)}, u32[]{:S(2)}) collective-permute-start(f32[3,1,384]{2,1,0:T(1,128)S(1)} %slice.41), channel_id=1, source_target_pairs={{0,1},{1,2},{2,3},{3,4},{4,5},{5,6},{6,7},{7,8},{8,9},{9,10},{10,1... | collective-permute-start | bytes 13832 | tf_op jit(solution)/shard_map/ppermute | solution.py:19
  (53 other events, 44.2 us)
Sparse Core Ops, SparseCore 0:
  9.8 151.4 all-gather.1
